TPU v7x, 32 devices: a whole 2x2x4 slice. The times are simulated.
32 devices in a mesh: blk: 8 (over z, x), deg: 4 (over y, core).
Axes of the slice: x: 2, y: 2, z: 4, core: 2. Of those that a mesh axis runs over, the one named last changes fastest.
Arguments:
- source: bfloat16 [672, 2048], P('deg', 'blk'), may hold values from -6 to 6
- operators: bfloat16 [12, 672, 672], replicated, may hold values from -0.125 to 0.125
- mie_factor: float32 [672, 2048], P('deg', 'blk'), may hold values from 0.3 to 1.5
- pair_source: int32 [6, 4, 2048], P(None, None, 'blk'), may hold values from 0 to 255
- pair_class: int32 [6, 4, 2048], P(None, None, 'blk'), may hold values from 0 to 11
- pair_scale: bfloat16 [6, 4, 2048], P(None, None, 'blk'), may hold values from 0.25 to 1
Outputs:
- result: float32 [672, 2048], P('deg', 'blk')
Inputs may be any that keep to these rules, and one draw needn't show every extreme that they name: `pair_source`: index of a source sphere within the visited block.
All inputs are finite; a program needn't handle non-finite values.
Results may differ from a plain program's by a relative error of at most 0.0075.
Values may be sent and summed in bfloat16 or wider, within the bound.
A program may use at most 64 MiB of HBM per device.

v0:
```python
import jax
import jax.numpy as jnp
from jax import lax
from jax.sharding import PartitionSpec as P


def from_behind(value, axis, steps):
    count = lax.axis_size(axis)
    pairs = [(source, (source + steps) % count) for source in range(count)]
    return lax.ppermute(value, axis, pairs)


def selection(indices, kinds, scales, classes, sphere_count):
    sphere_iota = jnp.arange(sphere_count, dtype=jnp.int32)[:, None, None]
    class_iota = jnp.arange(classes, dtype=jnp.int32)[None, :, None]
    table = jnp.zeros((sphere_count, classes, indices.shape[1]), jnp.float32)
    for slot in range(indices.shape[0]):
        hit = (indices[slot][None, None, :] == sphere_iota) & (
            kinds[slot][None, None, :] == class_iota
        )
        table = table + jnp.where(hit, scales[slot].astype(jnp.float32)[None, None, :], 0.0)
    return table.astype(jnp.bfloat16).reshape(sphere_count, classes * indices.shape[1])


def combine(visiting, table, classes):
    mixed = jnp.dot(visiting, table, preferred_element_type=jnp.float32)
    return mixed.astype(jnp.bfloat16).reshape(visiting.shape[0], classes, visiting.shape[1])


def local(source, operators, mie_factor, pair_source, pair_class, pair_scale):
    local_rows = source.shape[0]
    sphere_count = source.shape[1]
    classes = operators.shape[0]
    full_width = operators.shape[1]
    step_count = pair_source.shape[0]
    offset_start = lax.axis_index("deg") * local_rows
    weight_cols = lax.dynamic_slice_in_dim(operators, offset_start, local_rows, 2)
    weight_flat = jnp.transpose(weight_cols, (1, 2, 0)).reshape(full_width, local_rows * classes)
    target_field = jnp.zeros((full_width, sphere_count), jnp.float32)
    visiting = source
    for cycle_step in range(step_count):
        if cycle_step > 0:
            visiting = from_behind(source, "blk", cycle_step)
        table = selection(
            pair_source[cycle_step],
            pair_class[cycle_step],
            pair_scale[cycle_step],
            classes,
            sphere_count,
        )
        combined = combine(visiting, table, classes)
        operand = combined.reshape(combined.shape[0] * classes, sphere_count)
        target_field = target_field + jnp.dot(
            weight_flat, operand, preferred_element_type=jnp.float32
        )
    target_field = lax.psum_scatter(
        target_field.astype(jnp.bfloat16), "deg", scatter_dimension=0, tiled=True
    ).astype(jnp.float32)
    return source.astype(jnp.float32) - mie_factor * target_field


def solution(mesh):
    return jax.shard_map(
        local,
        mesh=mesh,
        in_specs=(
            P("deg", "blk"),
            P(),
            P("deg", "blk"),
            P(None, None, "blk"),
            P(None, None, "blk"),
            P(None, None, "blk"),
        ),
        out_specs=P("deg", "blk"),
        check_vma=False,
    )
```

profile of v0, /device:TPU:0, one launch (start us, length us, event | category | flops | bytes accessed | tf_op | source)
XLA Modules:
  0.0 128.8 jit_solution(7207513248908153394)
XLA Ops:
  6.5 3.0 %collective-permute-start = (bf16[168,256]{1,0:T(8,128)(2,1)}, bf16[168,256]{1,0:T(8,128)(2,1)S(1)}, u32[]{:S(2)}, u32[]{:S(2)}) collective-permute-start(bf16[168,256]{1,0:T(8,128)(2,1)} %param.6), channel_id=1, source_target_pairs={{0,4},{4,8},{8,12},{12,16},{16,20},{20,24},{24,28},{28,0},{1,5},{5... | collective-permute-start | bytes 258056 | tf_op jit(solution)/shard_map/ppermute | solution.py:10
  9.5 1.6 %collective-permute-start.1 = (bf16[168,256]{1,0:T(8,128)(2,1)}, bf16[168,256]{1,0:T(8,128)(2,1)S(1)}, u32[]{:S(2)}, u32[]{:S(2)}) collective-permute-start(bf16[168,256]{1,0:T(8,128)(2,1)} %param.6), channel_id=1, source_target_pairs={{0,8},{4,12},{8,16},{12,20},{16,24},{20,28},{24,0},{28,4},{1,9},{5... | collective-permute-start | bytes 258056 | tf_op jit(solution)/shard_map/ppermute | solution.py:10
  11.1 2.6 %collective-permute-start.2 = (bf16[168,256]{1,0:T(8,128)(2,1)}, bf16[168,256]{1,0:T(8,128)(2,1)S(1)}, u32[]{:S(2)}, u32[]{:S(2)}) collective-permute-start(bf16[168,256]{1,0:T(8,128)(2,1)} %param.6), channel_id=1, source_target_pairs={{0,12},{4,16},{8,20},{12,24},{16,28},{20,0},{24,4},{28,8},{1,13},{... | collective-permute-start | bytes 258056 | tf_op jit(solution)/shard_map/ppermute | solution.py:10
  13.6 1.2 collective-permute-start.3
  14.9 2.6 %collective-permute-start.4 = (bf16[168,256]{1,0:T(8,128)(2,1)}, bf16[168,256]{1,0:T(8,128)(2,1)S(1)}, u32[]{:S(2)}, u32[]{:S(2)}) collective-permute-start(bf16[168,256]{1,0:T(8,128)(2,1)} %param.6), channel_id=1, source_target_pairs={{0,20},{4,24},{8,28},{12,0},{16,4},{20,8},{24,12},{28,16},{1,21},{... | collective-permute-start | bytes 258056 | tf_op jit(solution)/shard_map/ppermute | solution.py:10
  17.5 0.9 slice_convert_fusion.3
  18.4 0.8 slice_convert_fusion.1
  19.2 0.9 fusion.9
  20.1 0.8 fusion.10
  20.9 0.9 fusion.7
  21.9 0.8 fusion.8
  22.7 6.9 %dynamic-slice_bitcast_fusion = bf16[672,168,12]{1,0,2:T(8,128)(2,1)} fusion(bf16[12,672,672]{2,1,0:T(8,128)(2,1)} %param.7, s32[]{:T(128)S(6)} %select_n.100), kind=kLoop, calls=%fused_computation | loop fusion | bytes 5419012 | tf_op jit(solution)/shard_map/transpose | solution.py:38
  29.6 7.2 %copy.7 = bf16[672,168,12]{0,2,1:T(8,128)(2,1)} copy(bf16[672,168,12]{1,0,2:T(8,128)(2,1)} %dynamic-slice_bitcast_fusion) | data formatting | bytes 5419008 | tf_op jit(solution)/shard_map/transpose | solution.py:38
  36.8 6.6 %reshape.1309 = bf16[672,2016]{0,1:T(8,128)(2,1)} reshape(bf16[672,168,12]{0,2,1:T(8,128)(2,1)} %copy.7) | data formatting | bytes 5419008 | tf_op jit(solution)/shard_map/reshape | solution.py:38
  43.6 0.1 iota_compare_fusion.20
  43.7 0.1 iota_compare_fusion.22
  43.9 3.7 %add_convert_fusion.5 = bf16[256,3072]{0,1:T(8,128)(2,1)S(1)} fusion(f32[3072]{0:T(1024)S(1)} %broadcast_in_dim.421, f32[3072]{0:T(1024)S(1)} %broadcast_in_dim.416, f32[3072]{0:T(1024)S(1)} %broadcast_in_dim.411, f32[3072]{0:T(1024)S(1)} %broadcast_in_dim.405, pred[3072]{0:T(1024)(128)(4,1)S(1)} %eq.1067, pred[3072]{0:T(1024)(128)(4,1)S(1)} %eq.1058, ...), kind=kLoop, calls=%fused_computation.18 | loop fusion | flops 9437184 | bytes 1896448 | tf_op jit(solution)/shard_map/convert_element_type | solution.py:22
  47.6 0.0 copy-done.5
  47.6 0.7 fusion
  48.2 1.2 reshape_reshape.18
  49.8 3.8 %fusion.11 = f32[672,256]{1,0:T(8,128)} fusion(bf16[672,2016]{0,1:T(8,128)(2,1)} %reshape.1309, bf16[2016,256]{1,0:T(8,128)(2,1)S(1)} %reshape_reshape.18), kind=kOutput, calls=%fused_computation.126 | convolution fusion | flops 693633024 | bytes 4429824 | tf_op jit(solution)/shard_map/dot_general | solution.py:53
  53.6 0.1 iota_compare_fusion.16
  53.7 0.1 iota_compare_fusion.18
  53.9 0.1 iota_compare_fusion.12
  54.0 0.1 iota_compare_fusion.14
  54.2 0.1 iota_compare_fusion.8
  54.3 0.1 iota_compare_fusion.10
  54.5 0.1 iota_compare_fusion.4
  54.6 0.1 iota_compare_fusion.6
  54.8 0.1 iota_compare_fusion
  54.9 0.1 iota_compare_fusion.2
  55.9 3.7 %add_convert_fusion.4 = bf16[256,3072]{0,1:T(8,128)(2,1)S(1)} fusion(f32[3072]{0:T(1024)S(1)} %broadcast_in_dim.441, f32[3072]{0:T(1024)S(1)} %broadcast_in_dim.436, f32[3072]{0:T(1024)S(1)} %broadcast_in_dim.431, f32[3072]{0:T(1024)S(1)} %broadcast_in_dim.426, pred[3072]{0:T(1024)(128)(4,1)S(1)} %eq.1103, pred[3072]{0:T(1024)(128)(4,1)S(1)} %eq.1094, ...), kind=kLoop, calls=%fused_computation.17 | loop fusion | flops 9437184 | bytes 1896448 | tf_op jit(solution)/shard_map/convert_element_type | solution.py:22
  59.6 3.7 %add_convert_fusion.3 = bf16[256,3072]{0,1:T(8,128)(2,1)S(1)} fusion(f32[3072]{0:T(1024)S(1)} %broadcast_in_dim.461, f32[3072]{0:T(1024)S(1)} %broadcast_in_dim.456, f32[3072]{0:T(1024)S(1)} %broadcast_in_dim.451, f32[3072]{0:T(1024)S(1)} %broadcast_in_dim.446, pred[3072]{0:T(1024)(128)(4,1)S(1)} %eq.1139, pred[3072]{0:T(1024)(128)(4,1)S(1)} %eq.1130, ...), kind=kLoop, calls=%fused_computation.16 | loop fusion | flops 9437184 | bytes 1896448 | tf_op jit(solution)/shard_map/convert_element_type | solution.py:22
  63.2 3.7 %add_convert_fusion.2 = bf16[256,3072]{0,1:T(8,128)(2,1)S(1)} fusion(f32[3072]{0:T(1024)S(1)} %broadcast_in_dim.481, f32[3072]{0:T(1024)S(1)} %broadcast_in_dim.476, f32[3072]{0:T(1024)S(1)} %broadcast_in_dim.471, f32[3072]{0:T(1024)S(1)} %broadcast_in_dim.466, pred[3072]{0:T(1024)(128)(4,1)S(1)} %eq.1175, pred[3072]{0:T(1024)(128)(4,1)S(1)} %eq.1166, ...), kind=kLoop, calls=%fused_computation.15 | loop fusion | flops 9437184 | bytes 1896448 | tf_op jit(solution)/shard_map/convert_element_type | solution.py:22
  66.9 3.7 %add_convert_fusion.1 = bf16[256,3072]{0,1:T(8,128)(2,1)S(1)} fusion(f32[3072]{0:T(1024)S(1)} %broadcast_in_dim.501, f32[3072]{0:T(1024)S(1)} %broadcast_in_dim.496, f32[3072]{0:T(1024)S(1)} %broadcast_in_dim.491, f32[3072]{0:T(1024)S(1)} %broadcast_in_dim.486, pred[3072]{0:T(1024)(128)(4,1)S(1)} %eq.1211, pred[3072]{0:T(1024)(128)(4,1)S(1)} %eq.1202, ...), kind=kLoop, calls=%fused_computation.14 | loop fusion | flops 9437184 | bytes 1896448 | tf_op jit(solution)/shard_map/convert_element_type | solution.py:22
  70.6 3.9 %add_convert_fusion = bf16[256,3072]{0,1:T(8,128)(2,1)S(1)} fusion(f32[3072]{0:T(1024)S(1)} %broadcast_in_dim.521, f32[3072]{0:T(1024)S(1)} %broadcast_in_dim.516, f32[3072]{0:T(1024)S(1)} %broadcast_in_dim.511, f32[3072]{0:T(1024)S(1)} %broadcast_in_dim.506, pred[3072]{0:T(1024)(128)(4,1)S(1)} %eq.1247, pred[3072]{0:T(1024)(128)(4,1)S(1)} %eq.1238, ...), kind=kLoop, calls=%fused_computation.13 | loop fusion | flops 9437184 | bytes 1896448 | tf_op jit(solution)/shard_map/convert_element_type | solution.py:22
  74.4 0.0 collective-permute-done
  74.5 0.7 fusion.1
  75.1 0.0 collective-permute-done.1
  75.1 1.7 %fusion.2 = bf16[168,3072]{1,0:T(8,128)(2,1)} fusion(bf16[256,3072]{0,1:T(8,128)(2,1)S(1)} %add_convert_fusion.3, bf16[168,256]{1,0:T(8,128)(2,1)S(1)} %collective-permute-done.1), kind=kOutput, calls=%fused_computation.9 | convolution fusion | flops 264757248 | bytes 2691072 | tf_op jit(solution)/shard_map/dot_general | solution.py:26
  76.8 0.0 collective-permute-done.2
  76.8 1.6 %fusion.3 = bf16[168,3072]{1,0:T(8,128)(2,1)} fusion(bf16[256,3072]{0,1:T(8,128)(2,1)S(1)} %add_convert_fusion.2, bf16[168,256]{1,0:T(8,128)(2,1)S(1)} %collective-permute-done.2), kind=kOutput, calls=%fused_computation.10 | convolution fusion | flops 264757248 | bytes 2691072 | tf_op jit(solution)/shard_map/dot_general | solution.py:26
  78.4 0.0 collective-permute-done.3
  78.4 1.7 %fusion.4 = bf16[168,3072]{1,0:T(8,128)(2,1)} fusion(bf16[256,3072]{0,1:T(8,128)(2,1)S(1)} %add_convert_fusion.1, bf16[168,256]{1,0:T(8,128)(2,1)S(1)} %collective-permute-done.3), kind=kOutput, calls=%fused_computation.11 | convolution fusion | flops 264757248 | bytes 2691072 | tf_op jit(solution)/shard_map/dot_general | solution.py:26
  80.2 2.1 %reshape_reshape.19 = bf16[2016,256]{1,0:T(8,128)(2,1)} reshape(bf16[168,3072]{1,0:T(8,128)(2,1)S(1)} %fusion.1) | data formatting | bytes 2064384 | tf_op jit(solution)/shard_map/reshape;reshape | solution.py:52
  82.3 3.2 %reshape_reshape.20 = bf16[2016,256]{1,0:T(8,128)(2,1)} reshape(bf16[168,3072]{1,0:T(8,128)(2,1)} %fusion.2) | data formatting | bytes 2064384 | tf_op jit(solution)/shard_map/reshape;reshape | solution.py:52
  85.6 3.1 %reshape_reshape.21 = bf16[2016,256]{1,0:T(8,128)(2,1)} reshape(bf16[168,3072]{1,0:T(8,128)(2,1)} %fusion.3) | data formatting | bytes 2064384 | tf_op jit(solution)/shard_map/reshape;reshape | solution.py:52
  88.7 2.1 %reshape_reshape.22 = bf16[2016,256]{1,0:T(8,128)(2,1)} reshape(bf16[168,3072]{1,0:T(8,128)(2,1)S(1)} %copy-done) | data formatting | bytes 2064384 | tf_op jit(solution)/shard_map/reshape;reshape | solution.py:52
  90.8 0.0 collective-permute-done.4
  90.8 0.7 fusion.5
  91.5 1.2 reshape_reshape.23
  92.8 3.3 %convolution_add_fusion.4 = f32[672,256]{1,0:T(8,128)S(1)} fusion(f32[672,256]{1,0:T(8,128)S(1)} %copy-done.7, bf16[672,2016]{0,1:T(8,128)(2,1)} %reshape.1309, bf16[2016,256]{1,0:T(8,128)(2,1)} %reshape_reshape.19), kind=kOutput, calls=%fused_computation.47 | convolution fusion | flops 693805056 | bytes 5117952 | tf_op jit(solution)/shard_map/dot_general | solution.py:53
  96.1 0.0 copy-done.1
  96.1 0.0 copy-done.4
  96.1 1.0 convolution_add_fusion.3
  97.2 0.2 copy-done.3
  97.4 1.0 convolution_add_fusion.2
  98.4 0.2 copy-done.2
  98.6 1.0 convolution_add_fusion.1
  99.6 0.0 copy-start.6
  99.6 1.9 %fusion.6 = bf16[672,256]{1,0:T(8,128)(2,1)} fusion(f32[672,256]{1,0:T(8,128)S(1)} %convolution_add_fusion.1, bf16[672,2016]{0,1:T(8,128)(2,1)S(1)} %copy-done.1, bf16[2016,256]{1,0:T(8,128)(2,1)S(1)} %reshape_reshape.23), kind=kOutput, calls=%fused_computation.48 | convolution fusion | flops 693977088 | bytes 4773888 | tf_op jit(solution)/shard_map/dot_general | solution.py:53
  101.5 0.0 reduce-scatter.2.cloned.1.call-update
  101.5 18.8 %reduce-scatter.2.cloned.1.call-done = bf16[168,256]{1,0:T(8,128)(2,1)} async-done(((bf16[672,256]{1,0:T(8,128)(2,1)}), bf16[168,256]{1,0:T(8,128)(2,1)}) %reduce-scatter.2.cloned.1.call-update) | async-done | bytes 86032 | tf_op jit(solution)/shard_map/reduce_scatter | solution.py:56
  120.3 1.6 %multiply_subtract_fusion = f32[168,256]{1,0:T(8,128)} fusion(f32[168,256]{1,0:T(8,128)S(1)} %copy-done.6, bf16[168,256]{1,0:T(8,128)(2,1)} %reduce-scatter.2.cloned.1.call-done, bf16[168,256]{1,0:T(8,128)(2,1)S(1)} %copy-done.5), kind=kLoop, calls=%fused_computation.73 | loop fusion | flops 172032 | bytes 516096 | tf_op jit(solution)/shard_map/sub | solution.py:59
  (107 shorter events, 0.6 us)
Async XLA Ops:
  6.5 113.8 %reduce-scatter.2.cloned.1.call-start = ((), (), s32[]{:S(2)}) async-start(), calls=%async_computation.1 | async-start | bytes 430080 | tf_op jit(solution)/shard_map/reduce_scatter | solution.py:56
  6.5 67.9 %collective-permute-start = (bf16[168,256]{1,0:T(8,128)(2,1)}, bf16[168,256]{1,0:T(8,128)(2,1)S(1)}, u32[]{:S(2)}, u32[]{:S(2)}) collective-permute-start(bf16[168,256]{1,0:T(8,128)(2,1)} %param.6), channel_id=1, source_target_pairs={{0,4},{4,8},{8,12},{12,16},{16,20},{20,24},{24,28},{28,0},{1,5},{5... | collective-permute-start | bytes 258056 | tf_op jit(solution)/shard_map/ppermute | solution.py:10
  9.5 65.6 %collective-permute-start.1 = (bf16[168,256]{1,0:T(8,128)(2,1)}, bf16[168,256]{1,0:T(8,128)(2,1)S(1)}, u32[]{:S(2)}, u32[]{:S(2)}) collective-permute-start(bf16[168,256]{1,0:T(8,128)(2,1)} %param.6), channel_id=1, source_target_pairs={{0,8},{4,12},{8,16},{12,20},{16,24},{20,28},{24,0},{28,4},{1,9},{5... | collective-permute-start | bytes 258056 | tf_op jit(solution)/shard_map/ppermute | solution.py:10
  11.1 65.7 %collective-permute-start.2 = (bf16[168,256]{1,0:T(8,128)(2,1)}, bf16[168,256]{1,0:T(8,128)(2,1)S(1)}, u32[]{:S(2)}, u32[]{:S(2)}) collective-permute-start(bf16[168,256]{1,0:T(8,128)(2,1)} %param.6), channel_id=1, source_target_pairs={{0,12},{4,16},{8,20},{12,24},{16,28},{20,0},{24,4},{28,8},{1,13},{... | collective-permute-start | bytes 258056 | tf_op jit(solution)/shard_map/ppermute | solution.py:10
  13.6 64.8 %collective-permute-start.3 = (bf16[168,256]{1,0:T(8,128)(2,1)}, bf16[168,256]{1,0:T(8,128)(2,1)S(1)}, u32[]{:S(2)}, u32[]{:S(2)}) collective-permute-start(bf16[168,256]{1,0:T(8,128)(2,1)} %param.6), channel_id=1, source_target_pairs={{0,16},{4,20},{8,24},{12,28},{16,0},{20,4},{24,8},{28,12},{1,17},{... | collective-permute-start | bytes 258056 | tf_op jit(solution)/shard_map/ppermute | solution.py:10
  14.9 76.0 %collective-permute-start.4 = (bf16[168,256]{1,0:T(8,128)(2,1)}, bf16[168,256]{1,0:T(8,128)(2,1)S(1)}, u32[]{:S(2)}, u32[]{:S(2)}) collective-permute-start(bf16[168,256]{1,0:T(8,128)(2,1)} %param.6), channel_id=1, source_target_pairs={{0,20},{4,24},{8,28},{12,0},{16,4},{20,8},{24,12},{28,16},{1,21},{... | collective-permute-start | bytes 258056 | tf_op jit(solution)/shard_map/ppermute | solution.py:10
  36.8 10.8 %copy-start.5 = (bf16[168,256]{1,0:T(8,128)(2,1)S(1)}, bf16[168,256]{1,0:T(8,128)(2,1)}, u32[]{:S(2)}) copy-start(bf16[168,256]{1,0:T(8,128)(2,1)} %param.6) | copy-start | bytes 258052
  82.3 6.4 %copy-start = (bf16[168,3072]{1,0:T(8,128)(2,1)S(1)}, bf16[168,3072]{1,0:T(8,128)(2,1)}, u32[]{:S(2)}) copy-start(bf16[168,3072]{1,0:T(8,128)(2,1)} %fusion.4) | copy-start | bytes 3096580
  88.7 4.1 %copy-start.7 = (f32[672,256]{1,0:T(8,128)S(1)}, f32[672,256]{1,0:T(8,128)}, u32[]{:S(2)}) copy-start(f32[672,256]{1,0:T(8,128)} %fusion.11) | copy-start | bytes 2064388
  92.8 3.4 %copy-start.1 = (bf16[672,2016]{0,1:T(8,128)(2,1)S(1)}, bf16[672,2016]{0,1:T(8,128)(2,1)}, u32[]{:S(2)}) copy-start(bf16[672,2016]{0,1:T(8,128)(2,1)} %reshape.1309) | copy-start | bytes 8128516
  92.8 3.4 %copy-start.4 = (bf16[2016,256]{1,0:T(8,128)(2,1)S(1)}, bf16[2016,256]{1,0:T(8,128)(2,1)}, u32[]{:S(2)}) copy-start(bf16[2016,256]{1,0:T(8,128)(2,1)} %reshape_reshape.20) | copy-start | bytes 3096580
  96.1 1.2 copy-start.3
  97.4 1.2 copy-start.2
  99.6 20.7 %copy-start.6 = (f32[168,256]{1,0:T(8,128)S(1)}, f32[168,256]{1,0:T(8,128)}, u32[]{:S(2)}) copy-start(f32[168,256]{1,0:T(8,128)} %param.8) | copy-start | bytes 516100
Sparse Core Ops, SparseCore 0:
  101.6 18.6 reduce-scatter.1
where the time goes:
time: 130 us; the launch traced here: 129 us
  local copies, waits for them, and re-layouts  38.1 us (29%)
  other arithmetic  27.3 us (21%)
  matrix products  19.2 us (15%)
  waiting for transfers between devices  18.8 us (14%)
  between operations  14.4 us (11%)
  starting transfers between devices  11 us (8%)
    convert_element_type x6, other arithmetic, selection(): table.astype(jnp.bfloat16).reshape(sphere_count, classes * indices.shape[1])  22.2 us
    reduce_scatter x1, waiting for transfers between devices, local(): lax.psum_scatter(target_field.astype(jnp.bfloat16), 'deg', scatter_dimens...  18.8 us
    transpose x2, local copies, waits for them, and re-layouts, local(): jnp.transpose(weight_cols, (1, 2, 0))  14.1 us
    another operation x6, local copies, waits for them, and re-layouts, local(): operand = combined.reshape(combined.shape[0] * classes, sphere_count)  13.1 us
    dot_general x6, matrix products, local(): jnp.dot(weight_flat, operand, preferred_element_type=jnp.float32)  12.1 us
    ppermute x5, starting transfers between devices, from_behind(): return lax.ppermute(value, axis, pairs)  11 us
    dot_general x6, matrix products, combine(): mixed = jnp.dot(visiting, table, preferred_element_type=jnp.float32)  7.05 us
    reshape x1, local copies, waits for them, and re-layouts, local(): jnp.transpose(weight_cols, (1, 2, 0))  6.63 us
  transfers between devices with their start and end apart: 6, of which 1 were waited for; matrix products, arithmetic and copies ran while one was open for 56% of the time, Pallas kernels for 0%

commit v1 on v0

v1 whole, which is shorter than its diff:
```python
import functools

import jax
import jax.numpy as jnp
from jax import lax
from jax.experimental import pallas as pl
from jax.experimental.pallas import tpu as pltpu
from jax.sharding import PartitionSpec as P

MESH = pl.DeviceIdType.MESH
LANES = 128


def window_of(rows, full, n_deg):
    lows = [position * rows // LANES * LANES for position in range(n_deg)]
    ends = [(position + 1) * rows - low for position, low in enumerate(lows)]
    main = min(-(-max(ends) // LANES) * LANES, full - lows[-1]) // LANES * LANES
    tail = full - lows[-1] - main
    assert max(ends[:-1]) <= main and 0 <= tail < LANES
    return main, tail


def kernel(
    n_blk,
    n_deg,
    source_ref,
    op_ref,
    mie_ref,
    index_ref,
    kind_ref,
    scale_ref,
    out_ref,
    visit,
    hot,
    acc,
    total,
    weights,
    send_buf,
    recv_buf,
    visit_send,
    visit_recv,
    field_send,
    field_recv,
    op_sem,
):
    rows, spheres = source_ref.shape
    classes, full, _ = op_ref.shape
    steps, slots, _ = index_ref.shape
    group = weights.shape[2] // rows
    n_groups = n_deg // group
    blk = lax.axis_index("blk")
    deg = lax.axis_index("deg")
    mine = deg // group

    main, tail = window_of(rows, full, n_deg)

    def op_copy(part):
        return pltpu.make_async_copy(
            op_ref.at[:, pl.ds(part * group * rows, group * rows), :],
            weights.at[part],
            op_sem.at[part],
        )

    for part in range(n_groups):
        op_copy(part).start()

    def partner(shift):
        inner = lax.rem(lax.rem(deg, group) + shift % group, group)
        outer = lax.rem(mine + shift // group, n_groups)
        return outer * group + inner

    barrier = pltpu.get_barrier_semaphore()
    for step in range(1, steps):
        pl.semaphore_signal(
            barrier, inc=1, device_id=(lax.rem(blk + n_blk - step, n_blk), deg), device_id_type=MESH
        )
    for shift in range(1, n_deg):
        pl.semaphore_signal(
            barrier, inc=1, device_id=(blk, lax.rem(deg + shift, n_deg)), device_id_type=MESH
        )
    pl.semaphore_wait(barrier, steps - 1 + n_deg - 1)

    def visit_copy(step):
        return pltpu.make_async_remote_copy(
            src_ref=source_ref,
            dst_ref=visit.at[step],
            send_sem=visit_send.at[step],
            recv_sem=visit_recv.at[step],
            device_id=(lax.rem(blk + step, n_blk), deg),
            device_id_type=MESH,
        )

    for step in range(1, steps):
        visit_copy(step).start()

    visit[0] = source_ref[...]
    acc[...] = jnp.zeros(acc.shape, acc.dtype)
    shift_rows = pl.multiple_of(lax.rem(deg * rows, LANES), 8)

    def one_visit(step, carry):
        sphere = lax.broadcasted_iota(jnp.int32, (spheres, spheres), 0)
        for slot in range(slots):
            row = index_ref[step, slot : slot + 1, :]
            hit = jnp.where(sphere == row, 1.0, 0.0).astype(jnp.bfloat16)
            hot[slot] = hit.reshape(hot.shape[1:])
        kinds = kind_ref[step]
        scales = scale_ref[step].astype(jnp.float32)

        @pl.when(step > 0)
        def _():
            visit_copy(step).wait_recv()

        value = visit[step]
        for kind in range(classes):
            weight = jnp.where(kinds == kind, scales, 0.0)
            table = None
            for slot in range(slots):
                line = jnp.broadcast_to(weight[slot : slot + 1, :], (16, spheres))
                term = hot[slot] * line.astype(jnp.bfloat16)[None]
                table = term if table is None else table + term
            part = jnp.dot(
                value, table.reshape(spheres, spheres), preferred_element_type=jnp.float32
            )
            acc[kind, pl.ds(shift_rows, rows), :] += part
        return carry

    lax.fori_loop(0, steps, one_visit, 0)

    for part in range(n_groups):
        op_copy(part).wait()
    low = pl.multiple_of(deg * rows // LANES * LANES, LANES)

    def field_copy(shift):
        target = partner(shift)
        return pltpu.make_async_remote_copy(
            src_ref=send_buf.at[shift],
            dst_ref=recv_buf.at[shift],
            send_sem=field_send.at[shift],
            recv_sem=field_recv.at[shift],
            device_id=(blk, target),
            device_id_type=MESH,
        )

    own = None
    for outer in list(range(1, n_groups)) + [0]:
        which = lax.rem(mine + outer, n_groups)
        field = None
        for kind in range(classes):
            term = jnp.dot(
                weights[which, kind, :, pl.ds(low, main)],
                acc[kind, :main, :].astype(jnp.bfloat16),
                preferred_element_type=jnp.float32,
            )
            if tail:
                term += jnp.dot(
                    weights[which, kind, :, full - tail :],
                    acc[kind, main:, :].astype(jnp.bfloat16),
                    preferred_element_type=jnp.float32,
                )
            field = term if field is None else field + term
        total[...] = field
        for inner in list(range(1, group)) + [0]:
            shift = outer * group + inner
            place = lax.rem(lax.rem(deg, group) + inner, group)
            piece = total[pl.ds(pl.multiple_of(place * rows, 8), rows), :]
            if shift == 0:
                own = piece
            else:
                send_buf[shift] = piece.astype(jnp.bfloat16)
                field_copy(shift).start()

    for shift in list(range(1, group)) + list(range(group, n_deg)):
        field_copy(shift).wait_recv()
        own = own + recv_buf[shift].astype(jnp.float32)
    out_ref[...] = source_ref[...].astype(jnp.float32) - mie_ref[...] * own
    for step in range(1, steps):
        visit_copy(step).wait_send()
    for shift in range(1, n_deg):
        field_copy(shift).wait_send()


def solution(mesh):
    n_blk = mesh.shape["blk"]
    n_deg = mesh.shape["deg"]

    def local(source, operators, mie_factor, pair_source, pair_class, pair_scale):
        rows, spheres = source.shape
        classes, full, _ = operators.shape
        steps, slots, _ = pair_source.shape
        group = 2 if n_deg % 2 == 0 else 1
        main, tail = window_of(rows, full, n_deg)
        vmem = pl.BlockSpec(memory_space=pltpu.VMEM)
        return pl.pallas_call(
            functools.partial(kernel, n_blk, n_deg),
            out_shape=jax.ShapeDtypeStruct((rows, spheres), jnp.float32),
            in_specs=[vmem, pl.BlockSpec(memory_space=pltpu.HBM), vmem, vmem, vmem, vmem],
            out_specs=vmem,
            scratch_shapes=[
                pltpu.VMEM((steps, rows, spheres), jnp.bfloat16),
                pltpu.VMEM((slots, spheres // 16, 16, spheres), jnp.bfloat16),
                pltpu.VMEM((classes, main + tail, spheres), jnp.float32),
                pltpu.VMEM((group * rows, spheres), jnp.float32),
                pltpu.VMEM((n_deg // group, classes, group * rows, full), jnp.bfloat16),
                pltpu.VMEM((n_deg, rows, spheres), jnp.bfloat16),
                pltpu.VMEM((n_deg, rows, spheres), jnp.bfloat16),
                pltpu.SemaphoreType.DMA((steps,)),
                pltpu.SemaphoreType.DMA((steps,)),
                pltpu.SemaphoreType.DMA((n_deg,)),
                pltpu.SemaphoreType.DMA((n_deg,)),
                pltpu.SemaphoreType.DMA((n_deg // group,)),
            ],
            compiler_params=pltpu.CompilerParams(
                collective_id=0, has_side_effects=True, vmem_limit_bytes=56 * 1024 * 1024
            ),
        )(source, operators, mie_factor, pair_source, pair_class, pair_scale)

    return jax.shard_map(
        local,
        mesh=mesh,
        in_specs=(
            P("deg", "blk"),
            P(),
            P("deg", "blk"),
            P(None, None, "blk"),
            P(None, None, "blk"),
            P(None, None, "blk"),
        ),
        out_specs=P("deg", "blk"),
        check_vma=False,
    )
```

time: 130 us -> 30.3 us (0.23)
  local copies, waits for them, and re-layouts: 38.1 us -> 1.6 us
  Pallas kernels: 0 us -> 28.6 us
  other arithmetic: 27.3 us -> 0 us
  matrix products: 19.2 us -> 0 us
  waiting for transfers between devices: 18.8 us -> 0 us
  between operations: 14.4 us -> 0.01 us
  starting transfers between devices: 11 us -> 0 us
    pallas_call x0 -> x1, Pallas kernels: none -> 28.6 us  [local(): pl.pallas_call(functools.partial(kernel, n_blk, n_deg), out_shape=jax.Sha...]
    convert_element_type x6 -> x0, other arithmetic: 22.2 us -> none  [selection(): table.astype(jnp.bfloat16).reshape(sphere_count, classes * indices.shape[1])]
    dot_general x12 -> x0, matrix products: 19.2 us -> none  [the longest x6 12.1 us: local(): jnp.dot(weight_flat, operand, preferred_element_type=jnp.float32)]
    reduce_scatter x1 -> x0, waiting for transfers between devices: 18.8 us -> none  [local(): lax.psum_scatter(target_field.astype(jnp.bfloat16), 'deg', scatter_dimens...]
    transpose x2 -> x0, local copies, waits for them, and re-layouts: 14.1 us -> none  [local(): jnp.transpose(weight_cols, (1, 2, 0))]
    another operation x6 -> x0, local copies, waits for them, and re-layouts: 13.1 us -> none  [local(): operand = combined.reshape(combined.shape[0] * classes, sphere_count)]
    ppermute x5 -> x0, starting transfers between devices: 11 us -> none  [from_behind(): return lax.ppermute(value, axis, pairs)]
    reshape x1 -> x0, local copies, waits for them, and re-layouts: 6.63 us -> none  [local(): jnp.transpose(weight_cols, (1, 2, 0))]
  transfers between devices with their start and end apart: 6 -> 0, of which waited for: 1 -> 0; matrix products, arithmetic and copies ran while one was open for 56% -> 0% of each run, Pallas kernels for 0% -> 0%
where the time goes in v1:
time: 30.3 us; the launch traced here: 30.2 us
  Pallas kernels  28.6 us (94%)
  local copies, waits for them, and re-layouts  1.6 us (5%)
    pallas_call x1, Pallas kernels, local(): pl.pallas_call(functools.partial(kernel, n_blk, n_deg), out_shape=jax.Sha...  28.6 us
    unnamed x1, local copies, waits for them, and re-layouts  1.6 us

profile of v1, /device:TPU:0, one launch (start us, length us, event | category | flops | bytes accessed | tf_op | source)
XLA Modules:
  0.0 30.2 jit_solution(2136110400343148788)
XLA Ops:
  0.0 28.6 %shard_map.64 = f32[168,256]{1,0:T(8,128)} custom-call(bf16[168,256]{1,0:T(8,128)(2,1)} %source_ref.1, bf16[12,672,672]{2,1,0:T(8,128)(2,1)} %op_ref.1, f32[168,256]{1,0:T(8,128)} %mie_ref.1, s32[6,4,256]{2,1,0:T(4,128)} %index_ref.1, s32[6,4,256]{2,1,0:T(4,128)} %kind_ref.1, bf16[6,4,256]{2,1,0:T(4,128)(2,1)} %scale_ref.1), custom_call_target="tpu_custom_call" | custom-call | tf_op jit(solution)/shard_map/pallas_call | solution.py:193
  28.6 1.6 %copy.8 = f32[168,256]{1,0:T(8,128)} copy(f32[168,256]{1,0:T(8,128)} %shard_map.64) | data formatting | bytes 344064

commit v2 on v1

--- a/solution.py
+++ b/solution.py
@@ -9,6 +9,7 @@
 
 MESH = pl.DeviceIdType.MESH
 LANES = 128
+PIECES = 2
 
 
 def window_of(rows, full, n_deg):
@@ -69,35 +70,56 @@
         outer = lax.rem(mine + shift // group, n_groups)
         return outer * group + inner
 
+    side = lax.rem(blk, 2)
+    ahead = (steps - 1) // 2
+    first_slot = 1 + side * (steps - 2)
+
+    def to_blk(shift):
+        return (lax.rem(blk + shift + n_blk, n_blk), deg)
+
     barrier = pltpu.get_barrier_semaphore()
-    for step in range(1, steps):
-        pl.semaphore_signal(
-            barrier, inc=1, device_id=(lax.rem(blk + n_blk - step, n_blk), deg), device_id_type=MESH
-        )
+    for source_of in (-2, 1 - 2 * side, side * (steps - 2) - (steps - 1)):
+        pl.semaphore_signal(barrier, inc=1, device_id=to_blk(source_of), device_id_type=MESH)
     for shift in range(1, n_deg):
         pl.semaphore_signal(
             barrier, inc=1, device_id=(blk, lax.rem(deg + shift, n_deg)), device_id_type=MESH
         )
-    pl.semaphore_wait(barrier, steps - 1 + n_deg - 1)
-
-    def visit_copy(step):
-        return pltpu.make_async_remote_copy(
-            src_ref=source_ref,
-            dst_ref=visit.at[step],
-            send_sem=visit_send.at[step],
-            recv_sem=visit_recv.at[step],
-            device_id=(lax.rem(blk + step, n_blk), deg),
-            device_id_type=MESH,
-        )
-
-    for step in range(1, steps):
-        visit_copy(step).start()
+    pl.semaphore_wait(barrier, 3 + n_deg - 1)
+
+    def move(src, slot, target, kind):
+        copies = []
+        width = spheres // PIECES
+        for piece in range(PIECES):
+            lanes = pl.ds(piece * width, width)
+            copies.append(
+                pltpu.make_async_remote_copy(
+                    src_ref=src.at[:, lanes],
+                    dst_ref=visit.at[slot, :, lanes],
+                    send_sem=visit_send.at[kind, piece],
+                    recv_sem=visit_recv.at[slot, piece],
+                    device_id=to_blk(target),
+                    device_id_type=MESH,
+                )
+            )
+        return copies
+
+    def direct():
+        return move(source_ref, first_slot, first_slot, 0)
+
+    def along(hop, src):
+        return move(src, 2 * hop, 2, hop)
+
+    def across(hop):
+        return move(visit.at[2 * hop], 2 * hop + 1 - 2 * side, 1 - 2 * side, ahead + hop)
+
+    for copy in along(1, source_ref) + direct():
+        copy.start()
 
     visit[0] = source_ref[...]
     acc[...] = jnp.zeros(acc.shape, acc.dtype)
     shift_rows = pl.multiple_of(lax.rem(deg * rows, LANES), 8)
 
-    def one_visit(step, carry):
+    def one_visit(step):
         sphere = lax.broadcasted_iota(jnp.int32, (spheres, spheres), 0)
         for slot in range(slots):
             row = index_ref[step, slot : slot + 1, :]
@@ -105,11 +127,6 @@
             hot[slot] = hit.reshape(hot.shape[1:])
         kinds = kind_ref[step]
         scales = scale_ref[step].astype(jnp.float32)
-
-        @pl.when(step > 0)
-        def _():
-            visit_copy(step).wait_recv()
-
         value = visit[step]
         for kind in range(classes):
             weight = jnp.where(kinds == kind, scales, 0.0)
@@ -122,9 +139,31 @@
                 value, table.reshape(spheres, spheres), preferred_element_type=jnp.float32
             )
             acc[kind, pl.ds(shift_rows, rows), :] += part
+
+    def two_visits(turn, carry):
+        one_visit(2 * turn)
+
+        @pl.when(turn < ahead)
+        def _():
+            arrived = move(source_ref, 2 * turn + 2, 2, 0)
+            onward = along(turn + 2, visit.at[2 * turn + 2])
+            over = across(turn + 1)
+            for piece in range(PIECES):
+                arrived[piece].wait_recv()
+
+                @pl.when(turn + 1 < ahead)
+                def _():
+                    onward[piece].start()
+
+                over[piece].start()
+
+        odd = lax.rem(2 * turn - 1 + 2 * side + steps, steps)
+        for copy in move(source_ref, odd, 2, 0):
+            copy.wait_recv()
+        one_visit(odd)
         return carry
 
-    lax.fori_loop(0, steps, one_visit, 0)
+    lax.fori_loop(0, steps // 2, two_visits, 0)
 
     for part in range(n_groups):
         op_copy(part).wait()
@@ -173,8 +212,11 @@
         field_copy(shift).wait_recv()
         own = own + recv_buf[shift].astype(jnp.float32)
     out_ref[...] = source_ref[...].astype(jnp.float32) - mie_ref[...] * own
-    for step in range(1, steps):
-        visit_copy(step).wait_send()
+    sent = direct()
+    for hop in range(1, ahead + 1):
+        sent += along(hop, source_ref) + across(hop)
+    for copy in sent:
+        copy.wait_send()
     for shift in range(1, n_deg):
         field_copy(shift).wait_send()
 
@@ -203,8 +245,8 @@
                 pltpu.VMEM((n_deg // group, classes, group * rows, full), jnp.bfloat16),
                 pltpu.VMEM((n_deg, rows, spheres), jnp.bfloat16),
                 pltpu.VMEM((n_deg, rows, spheres), jnp.bfloat16),
-                pltpu.SemaphoreType.DMA((steps,)),
-                pltpu.SemaphoreType.DMA((steps,)),
+                pltpu.SemaphoreType.DMA((2 * ((steps - 1) // 2) + 1, PIECES)),
+                pltpu.SemaphoreType.DMA((steps, PIECES)),
                 pltpu.SemaphoreType.DMA((n_deg,)),
                 pltpu.SemaphoreType.DMA((n_deg,)),
                 pltpu.SemaphoreType.DMA((n_deg // group,)),

time: 30.3 us -> 27.5 us (0.908)
  Pallas kernels: 28.6 us -> 25.8 us
    pallas_call x1, Pallas kernels: 28.6 us -> 25.8 us  [local(): pl.pallas_call(functools.partial(kernel, n_blk, n_deg), out_shape=jax.Sha...]
where the time goes in v2:
time: 27.5 us; the launch traced here: 27.4 us
  Pallas kernels  25.8 us (94%)
  local copies, waits for them, and re-layouts  1.6 us (6%)
    pallas_call x1, Pallas kernels, local(): pl.pallas_call(functools.partial(kernel, n_blk, n_deg), out_shape=jax.Sha...  25.8 us
    unnamed x1, local copies, waits for them, and re-layouts  1.6 us

profile of v2, /device:TPU:0, one launch (start us, length us, event | category | flops | bytes accessed | tf_op | source)
XLA Modules:
  0.0 27.4 jit_solution(2863906441722771352)
XLA Ops:
  0.0 25.8 %shard_map.64 = f32[168,256]{1,0:T(8,128)} custom-call(bf16[168,256]{1,0:T(8,128)(2,1)} %source_ref.1, bf16[12,672,672]{2,1,0:T(8,128)(2,1)} %op_ref.1, f32[168,256]{1,0:T(8,128)} %mie_ref.1, s32[6,4,256]{2,1,0:T(4,128)} %index_ref.1, s32[6,4,256]{2,1,0:T(4,128)} %kind_ref.1, bf16[6,4,256]{2,1,0:T(4,128)(2,1)} %scale_ref.1), custom_call_target="tpu_custom_call" | custom-call | tf_op jit(solution)/shard_map/pallas_call | solution.py:235
  25.8 1.6 %copy.8 = f32[168,256]{1,0:T(8,128)} copy(f32[168,256]{1,0:T(8,128)} %shard_map.64) | data formatting | bytes 344064

commit v3 on v2

--- a/solution.py
+++ b/solution.py
@@ -9,7 +9,7 @@
 
 MESH = pl.DeviceIdType.MESH
 LANES = 128
-PIECES = 2
+PIECES = 3
 
 
 def window_of(rows, full, n_deg):
@@ -21,16 +21,25 @@
     return main, tail
 
 
+def pieces_of(rows):
+    return next(count for count in (PIECES, 2, 1) if rows % (8 * count) == 0)
+
+
 def kernel(
     n_blk,
     n_deg,
     source_ref,
     op_ref,
+    mie_hbm,
+    index_hbm,
+    kind_hbm,
+    scale_hbm,
+    out_ref,
     mie_ref,
     index_ref,
     kind_ref,
     scale_ref,
-    out_ref,
+    in_sem,
     visit,
     hot,
     acc,
@@ -55,6 +64,21 @@
 
     main, tail = window_of(rows, full, n_deg)
 
+    fetches = [
+        pltpu.make_async_copy(src, dst, in_sem.at[which])
+        for which, (src, dst) in enumerate(
+            (
+                (source_ref, visit.at[0]),
+                (index_hbm, index_ref),
+                (kind_hbm, kind_ref),
+                (scale_hbm, scale_ref),
+                (mie_hbm, mie_ref),
+            )
+        )
+    ]
+    for fetch in fetches:
+        fetch.start()
+
     def op_copy(part):
         return pltpu.make_async_copy(
             op_ref.at[:, pl.ds(part * group * rows, group * rows), :],
@@ -62,8 +86,6 @@
             op_sem.at[part],
         )
 
-    for part in range(n_groups):
-        op_copy(part).start()
 
     def partner(shift):
         inner = lax.rem(lax.rem(deg, group) + shift % group, group)
@@ -72,6 +94,7 @@
 
     side = lax.rem(blk, 2)
     ahead = (steps - 1) // 2
+    pieces = pieces_of(rows)
     first_slot = 1 + side * (steps - 2)
 
     def to_blk(shift):
@@ -88,13 +111,13 @@
 
     def move(src, slot, target, kind):
         copies = []
-        width = spheres // PIECES
-        for piece in range(PIECES):
-            lanes = pl.ds(piece * width, width)
+        height = rows // pieces
+        for piece in range(pieces):
+            part = pl.ds(piece * height, height)
             copies.append(
                 pltpu.make_async_remote_copy(
-                    src_ref=src.at[:, lanes],
-                    dst_ref=visit.at[slot, :, lanes],
+                    src_ref=src.at[part],
+                    dst_ref=visit.at[slot, part],
                     send_sem=visit_send.at[kind, piece],
                     recv_sem=visit_recv.at[slot, piece],
                     device_id=to_blk(target),
@@ -114,8 +137,9 @@
 
     for copy in along(1, source_ref) + direct():
         copy.start()
-
-    visit[0] = source_ref[...]
+    for part in range(n_groups):
+        op_copy(part).start()
+
     acc[...] = jnp.zeros(acc.shape, acc.dtype)
     shift_rows = pl.multiple_of(lax.rem(deg * rows, LANES), 8)
 
@@ -140,30 +164,40 @@
             )
             acc[kind, pl.ds(shift_rows, rows), :] += part
 
-    def two_visits(turn, carry):
-        one_visit(2 * turn)
-
-        @pl.when(turn < ahead)
+    def take_turn(turn, carry):
+        last = 2 * ahead + 1
+        even = lax.rem(turn, 2) * (1 - turn // last)
+        behind = (turn - 1 + steps) // 2 - steps // 2
+        odd = lax.rem(2 * behind - 1 + 2 * side + 2 * steps, steps)
+        moved = (turn + last - 1) // last
+        step = moved * (even * (turn + 1) + (1 - even) * odd)
+
+        @pl.when(even == 1)
         def _():
-            arrived = move(source_ref, 2 * turn + 2, 2, 0)
-            onward = along(turn + 2, visit.at[2 * turn + 2])
-            over = across(turn + 1)
-            for piece in range(PIECES):
+            hop = (turn + 1) // 2
+            arrived = move(source_ref, 2 * hop, 2, 0)
+            onward = along(hop + 1, visit.at[2 * hop])
+            over = across(hop)
+            for piece in range(pieces):
                 arrived[piece].wait_recv()
 
-                @pl.when(turn + 1 < ahead)
+                @pl.when(hop < ahead)
                 def _():
                     onward[piece].start()
 
                 over[piece].start()
 
-        odd = lax.rem(2 * turn - 1 + 2 * side + steps, steps)
-        for copy in move(source_ref, odd, 2, 0):
-            copy.wait_recv()
-        one_visit(odd)
+        @pl.when(moved * (1 - even) == 1)
+        def _():
+            for copy in move(source_ref, odd, 2, 0):
+                copy.wait_recv()
+
+        one_visit(step)
         return carry
 
-    lax.fori_loop(0, steps // 2, two_visits, 0)
+    for fetch in fetches:
+        fetch.wait()
+    lax.fori_loop(0, steps, take_turn, 0)
 
     for part in range(n_groups):
         op_copy(part).wait()
@@ -211,7 +245,7 @@
     for shift in list(range(1, group)) + list(range(group, n_deg)):
         field_copy(shift).wait_recv()
         own = own + recv_buf[shift].astype(jnp.float32)
-    out_ref[...] = source_ref[...].astype(jnp.float32) - mie_ref[...] * own
+    out_ref[...] = visit[0].astype(jnp.float32) - mie_ref[...] * own
     sent = direct()
     for hop in range(1, ahead + 1):
         sent += along(hop, source_ref) + across(hop)
@@ -235,9 +269,14 @@
         return pl.pallas_call(
             functools.partial(kernel, n_blk, n_deg),
             out_shape=jax.ShapeDtypeStruct((rows, spheres), jnp.float32),
-            in_specs=[vmem, pl.BlockSpec(memory_space=pltpu.HBM), vmem, vmem, vmem, vmem],
+            in_specs=[pl.BlockSpec(memory_space=pltpu.HBM)] * 6,
             out_specs=vmem,
             scratch_shapes=[
+                pltpu.VMEM((rows, spheres), jnp.float32),
+                pltpu.VMEM(pair_source.shape, pair_source.dtype),
+                pltpu.VMEM(pair_class.shape, pair_class.dtype),
+                pltpu.VMEM(pair_scale.shape, pair_scale.dtype),
+                pltpu.SemaphoreType.DMA((5,)),
                 pltpu.VMEM((steps, rows, spheres), jnp.bfloat16),
                 pltpu.VMEM((slots, spheres // 16, 16, spheres), jnp.bfloat16),
                 pltpu.VMEM((classes, main + tail, spheres), jnp.float32),
@@ -245,8 +284,8 @@
                 pltpu.VMEM((n_deg // group, classes, group * rows, full), jnp.bfloat16),
                 pltpu.VMEM((n_deg, rows, spheres), jnp.bfloat16),
                 pltpu.VMEM((n_deg, rows, spheres), jnp.bfloat16),
-                pltpu.SemaphoreType.DMA((2 * ((steps - 1) // 2) + 1, PIECES)),
-                pltpu.SemaphoreType.DMA((steps, PIECES)),
+                pltpu.SemaphoreType.DMA((2 * ((steps - 1) // 2) + 1, pieces_of(rows))),
+                pltpu.SemaphoreType.DMA((steps, pieces_of(rows))),
                 pltpu.SemaphoreType.DMA((n_deg,)),
                 pltpu.SemaphoreType.DMA((n_deg,)),
                 pltpu.SemaphoreType.DMA((n_deg // group,)),

time: 27.5 us -> 26.7 us (0.971)
  Pallas kernels: 25.8 us -> 25 us
    pallas_call x1, Pallas kernels: 25.8 us -> 25 us  [local(): pl.pallas_call(functools.partial(kernel, n_blk, n_deg), out_shape=jax.Sha...]
where the time goes in v3:
time: 26.7 us; the launch traced here: 26.6 us
  Pallas kernels  25 us (94%)
  local copies, waits for them, and re-layouts  1.6 us (6%)
    pallas_call x1, Pallas kernels, local(): pl.pallas_call(functools.partial(kernel, n_blk, n_deg), out_shape=jax.Sha...  25 us
    unnamed x1, local copies, waits for them, and re-layouts  1.6 us

profile of v3, /device:TPU:0, one launch (start us, length us, event | category | flops | bytes accessed | tf_op | source)
XLA Modules:
  0.0 26.6 jit_solution(11737058723926927980)
XLA Ops:
  0.0 25.0 %shard_map.64 = f32[168,256]{1,0:T(8,128)} custom-call(bf16[168,256]{1,0:T(8,128)(2,1)} %source_ref.1, bf16[12,672,672]{2,1,0:T(8,128)(2,1)} %op_ref.1, f32[168,256]{1,0:T(8,128)} %mie_hbm.1, s32[6,4,256]{2,1,0:T(4,128)} %index_hbm.1, s32[6,4,256]{2,1,0:T(4,128)} %kind_hbm.1, bf16[6,4,256]{2,1,0:T(4,128)(2,1)} %scale_hbm.1), custom_call_target="tpu_custom_call" | custom-call | tf_op jit(solution)/shard_map/pallas_call | solution.py:269
  25.0 1.6 %copy.8 = f32[168,256]{1,0:T(8,128)} copy(f32[168,256]{1,0:T(8,128)} %shard_map.64) | data formatting | bytes 344064

commit v4 on v3

--- a/solution.py
+++ b/solution.py
@@ -43,7 +43,6 @@
     visit,
     hot,
     acc,
-    total,
     weights,
     send_buf,
     recv_buf,
@@ -56,7 +55,7 @@
     rows, spheres = source_ref.shape
     classes, full, _ = op_ref.shape
     steps, slots, _ = index_ref.shape
-    group = weights.shape[2] // rows
+    group = 2 if n_deg % 2 == 0 else 1
     n_groups = n_deg // group
     blk = lax.axis_index("blk")
     deg = lax.axis_index("deg")
@@ -81,16 +80,11 @@
 
     def op_copy(part):
         return pltpu.make_async_copy(
-            op_ref.at[:, pl.ds(part * group * rows, group * rows), :],
+            op_ref.at[:, pl.ds(part * rows, rows), :],
             weights.at[part],
             op_sem.at[part],
         )
 
-
-    def partner(shift):
-        inner = lax.rem(lax.rem(deg, group) + shift % group, group)
-        outer = lax.rem(mine + shift // group, n_groups)
-        return outer * group + inner
 
     side = lax.rem(blk, 2)
     ahead = (steps - 1) // 2
@@ -137,7 +131,7 @@
 
     for copy in along(1, source_ref) + direct():
         copy.start()
-    for part in range(n_groups):
+    for part in range(n_deg):
         op_copy(part).start()
 
     acc[...] = jnp.zeros(acc.shape, acc.dtype)
@@ -199,60 +193,72 @@
         fetch.wait()
     lax.fori_loop(0, steps, take_turn, 0)
 
-    for part in range(n_groups):
+    for part in range(n_deg):
         op_copy(part).wait()
     low = pl.multiple_of(deg * rows // LANES * LANES, LANES)
 
-    def field_copy(shift):
-        target = partner(shift)
+    core = lax.rem(deg, group)
+
+    def field_copy(slot, target):
         return pltpu.make_async_remote_copy(
-            src_ref=send_buf.at[shift],
-            dst_ref=recv_buf.at[shift],
-            send_sem=field_send.at[shift],
-            recv_sem=field_recv.at[shift],
+            src_ref=send_buf.at[slot],
+            dst_ref=recv_buf.at[slot],
+            send_sem=field_send.at[slot],
+            recv_sem=field_recv.at[slot],
             device_id=(blk, target),
             device_id_type=MESH,
         )
 
-    own = None
-    for outer in list(range(1, n_groups)) + [0]:
-        which = lax.rem(mine + outer, n_groups)
+    def to_pair(outer):
+        return field_copy(outer, mine * group + lax.rem(core + 1, group))
+
+    def to_far(outer):
+        return field_copy(n_groups + outer, lax.rem(mine + outer, n_groups) * group + core)
+
+    def field_of(owner):
         field = None
         for kind in range(classes):
             term = jnp.dot(
-                weights[which, kind, :, pl.ds(low, main)],
+                weights[owner, kind, :, pl.ds(low, main)],
                 acc[kind, :main, :].astype(jnp.bfloat16),
                 preferred_element_type=jnp.float32,
             )
             if tail:
                 term += jnp.dot(
-                    weights[which, kind, :, full - tail :],
+                    weights[owner, kind, :, full - tail :],
                     acc[kind, main:, :].astype(jnp.bfloat16),
                     preferred_element_type=jnp.float32,
                 )
             field = term if field is None else field + term
-        total[...] = field
-        for inner in list(range(1, group)) + [0]:
-            shift = outer * group + inner
-            place = lax.rem(lax.rem(deg, group) + inner, group)
-            piece = total[pl.ds(pl.multiple_of(place * rows, 8), rows), :]
-            if shift == 0:
-                own = piece
-            else:
-                send_buf[shift] = piece.astype(jnp.bfloat16)
-                field_copy(shift).start()
-
-    for shift in list(range(1, group)) + list(range(group, n_deg)):
-        field_copy(shift).wait_recv()
-        own = own + recv_buf[shift].astype(jnp.float32)
+        return field
+
+    started = []
+    for outer in list(range(1, n_groups)) + [0]:
+        first = lax.rem(mine + outer, n_groups) * group
+        if group > 1:
+            send_buf[outer] = field_of(first + lax.rem(core + 1, group)).astype(jnp.bfloat16)
+            to_pair(outer).start()
+            started.append(to_pair(outer))
+        own = field_of(first + core)
+        if group > 1:
+            to_pair(outer).wait_recv()
+            own = own + recv_buf[outer].astype(jnp.float32)
+        if outer > 0:
+            send_buf[n_groups + outer] = own.astype(jnp.bfloat16)
+            to_far(outer).start()
+            started.append(to_far(outer))
+
+    for outer in range(1, n_groups):
+        to_far(outer).wait_recv()
+        own = own + recv_buf[n_groups + outer].astype(jnp.float32)
     out_ref[...] = visit[0].astype(jnp.float32) - mie_ref[...] * own
     sent = direct()
     for hop in range(1, ahead + 1):
         sent += along(hop, source_ref) + across(hop)
     for copy in sent:
         copy.wait_send()
-    for shift in range(1, n_deg):
-        field_copy(shift).wait_send()
+    for copy in started:
+        copy.wait_send()
 
 
 def solution(mesh):
@@ -280,15 +286,14 @@
                 pltpu.VMEM((steps, rows, spheres), jnp.bfloat16),
                 pltpu.VMEM((slots, spheres // 16, 16, spheres), jnp.bfloat16),
                 pltpu.VMEM((classes, main + tail, spheres), jnp.float32),
-                pltpu.VMEM((group * rows, spheres), jnp.float32),
-                pltpu.VMEM((n_deg // group, classes, group * rows, full), jnp.bfloat16),
-                pltpu.VMEM((n_deg, rows, spheres), jnp.bfloat16),
-                pltpu.VMEM((n_deg, rows, spheres), jnp.bfloat16),
+                pltpu.VMEM((n_deg, classes, rows, full), jnp.bfloat16),
+                pltpu.VMEM((2 * (n_deg // group), rows, spheres), jnp.bfloat16),
+                pltpu.VMEM((2 * (n_deg // group), rows, spheres), jnp.bfloat16),
                 pltpu.SemaphoreType.DMA((2 * ((steps - 1) // 2) + 1, pieces_of(rows))),
                 pltpu.SemaphoreType.DMA((steps, pieces_of(rows))),
+                pltpu.SemaphoreType.DMA((2 * (n_deg // group),)),
+                pltpu.SemaphoreType.DMA((2 * (n_deg // group),)),
                 pltpu.SemaphoreType.DMA((n_deg,)),
-                pltpu.SemaphoreType.DMA((n_deg,)),
-                pltpu.SemaphoreType.DMA((n_deg // group,)),
             ],
             compiler_params=pltpu.CompilerParams(
                 collective_id=0, has_side_effects=True, vmem_limit_bytes=56 * 1024 * 1024

time: 26.7 us -> 26.3 us (0.985)
  Pallas kernels: 25 us -> 24.5 us
    pallas_call x1, Pallas kernels: 25 us -> 24.5 us  [local(): pl.pallas_call(functools.partial(kernel, n_blk, n_deg), out_shape=jax.Sha...]
where the time goes in v4:
time: 26.3 us; the launch traced here: 26.1 us
  Pallas kernels  24.5 us (93%)
  local copies, waits for them, and re-layouts  1.6 us (6%)
    pallas_call x1, Pallas kernels, local(): pl.pallas_call(functools.partial(kernel, n_blk, n_deg), out_shape=jax.Sha...  24.5 us
    unnamed x1, local copies, waits for them, and re-layouts  1.6 us

profile of v4, /device:TPU:0, one launch (start us, length us, event | category | flops | bytes accessed | tf_op | source)
XLA Modules:
  0.0 26.1 jit_solution(17932337895496618787)
XLA Ops:
  0.0 24.5 %shard_map.64 = f32[168,256]{1,0:T(8,128)} custom-call(bf16[168,256]{1,0:T(8,128)(2,1)} %source_ref.1, bf16[12,672,672]{2,1,0:T(8,128)(2,1)} %op_ref.1, f32[168,256]{1,0:T(8,128)} %mie_hbm.1, s32[6,4,256]{2,1,0:T(4,128)} %index_hbm.1, s32[6,4,256]{2,1,0:T(4,128)} %kind_hbm.1, bf16[6,4,256]{2,1,0:T(4,128)(2,1)} %scale_hbm.1), custom_call_target="tpu_custom_call" | custom-call | tf_op jit(solution)/shard_map/pallas_call | solution.py:275
  24.5 1.6 %copy.8 = f32[168,256]{1,0:T(8,128)} copy(f32[168,256]{1,0:T(8,128)} %shard_map.64) | data formatting | bytes 344064
